TPU v7x, 32 devices: a whole 2x2x4 slice. The times are simulated.
32 devices in a mesh: dp: 8 (over y, x, core), gz: 4 (over z).
Axes of the slice: x: 2, y: 2, z: 4, core: 2. Of those that a mesh axis runs over, the one named last changes fastest.
Arguments:
- volume: bfloat16 [8, 8, 32, 32, 128], P('dp', 'gz'), may hold values from -6 to 6
- cotangent: bfloat16 [8, 4, 16, 16, 256], P('dp', 'gz'), may hold values from -48 to 48
- weight: float32 [8, 27, 128, 256], P('dp'), may hold values from -6 to 6
- bias: float32 [8, 256], P('dp'), may hold values from -3 to 3
- exponent: int32 [4], replicated, may hold values from 0 to 2
Outputs:
- new_weight: float32 [8, 27, 128, 256], P('dp')
- new_bias: float32 [8, 256], P('dp')
- input_grad: bfloat16 [8, 8, 32, 32, 128], P('dp', 'gz')
All inputs are finite; a program needn't handle non-finite values.
Results may differ from a plain program's by a relative error of at most 0.0062.
Values may be sent and summed in bfloat16 or wider, within the bound.
No kernel may reach another device: no remote copies, remote signals or barrier semaphores. Data moves between devices by JAX's collectives and lax.ppermute only.
A program may use at most 128 MiB of HBM per device.

v0:
```python
from functools import partial
import math

import jax
import jax.numpy as jnp
from jax import lax
from jax.sharding import PartitionSpec as P

learning_rate = 0.5
cubic = 0.044715


def from_partner(block, axis, bit):
    count = lax.axis_size(axis)
    route = []
    for low in range(count):
        high = low | 1 << bit
        if high != low and high < count:
            route += [(low, high), (high, low)]
    return lax.ppermute(block, axis, route)


def extended(value, sides, width):
    for axis, dim in sides:
        devices, length = (lax.axis_size(axis), value.shape[dim])
        up = [(i, (i + 1) % devices) for i in range(devices - 1)]
        down = [(j, i) for i, j in up]
        last = lax.slice_in_dim(value, length - width, length, axis=dim)
        initial = lax.slice_in_dim(value, 0, width, axis=dim)
        before = lax.ppermute(last, axis, up)
        after = lax.ppermute(initial, axis, down)
        value = jnp.concatenate([before, value, after], axis=dim)
    return value


def gelu_slope(values):
    factor = math.sqrt(2.0 / math.pi)
    inner_arg = factor * (values + cubic * values * values * values)
    tangent = jnp.tanh(inner_arg)
    return 0.5 * (1.0 + tangent) + 0.5 * values * (1.0 - tangent * tangent) * factor * (
        1.0 + 3.0 * cubic * values * values
    )


def plane_patches(padded, plane_width):
    return jnp.concatenate(
        [
            padded[:, row_off : row_off + plane_width, col_off : col_off + plane_width, :]
            for row_off in range(3)
            for col_off in range(3)
        ],
        axis=3,
    )


def forward_terms(padded, low_three, planes, plane_width):
    patches = plane_patches(padded, plane_width)
    cell_count = planes * plane_width * plane_width
    preact = jnp.zeros((cell_count, low_three.shape[2]), jnp.float32)
    for depth_off in range(3):
        flat = patches[depth_off : depth_off + planes].reshape(cell_count, -1)
        preact = preact + jnp.dot(flat, low_three[depth_off], preferred_element_type=jnp.float32)
    return (patches, preact)


def weight_terms(patches, grad_pre, planes, plane_width, in_channels):
    cell_count = planes * plane_width * plane_width
    blocks = []
    for depth_off in range(3):
        flat = patches[depth_off : depth_off + planes].reshape(cell_count, -1)
        blocks.append(jnp.dot(flat.T, grad_pre, preferred_element_type=jnp.float32))
    stacked = jnp.stack(blocks, axis=0)
    return stacked.reshape(27, in_channels, grad_pre.shape[1])


def input_terms(grad_pad, low_weight, planes, plane_width):
    cell_count = planes * plane_width * plane_width
    accumulated = jnp.zeros((cell_count, low_weight.shape[1]), jnp.float32)
    for depth_off in range(3):
        for row_off in range(3):
            pieces = jnp.concatenate(
                [
                    grad_pad[
                        2 - depth_off : 2 - depth_off + planes,
                        2 - row_off : 2 - row_off + plane_width,
                        2 - col_off : 2 - col_off + plane_width,
                        :,
                    ]
                    for col_off in range(3)
                ],
                axis=3,
            )
            kernel_block = jnp.concatenate(
                [low_weight[depth_off * 9 + row_off * 3 + col_off].T for col_off in range(3)],
                axis=0,
            )
            accumulated = accumulated + jnp.dot(
                pieces.reshape(cell_count, -1), kernel_block, preferred_element_type=jnp.float32
            )
    return accumulated


def spread_cotangent(cotangent, planes, plane_width, out_channels):
    widened = jnp.broadcast_to(
        cotangent.astype(jnp.float32)[:, None, :, None, :, None, :],
        (planes // 2, 2, plane_width // 2, 2, plane_width // 2, 2, out_channels),
    )
    return widened.reshape(planes * plane_width * plane_width, out_channels)


def share_swap(current_w, current_b, bit):
    return from_partner((current_w, current_b), "dp", bit)


def per_device(volume, cotangent, weight, bias, exponent):
    local_slab = volume[0]
    planes, plane_width, _, in_channels = local_slab.shape
    master = weight[0]
    master_bias = bias[0]
    tap_count = master.shape[0]
    out_channels = master.shape[2]
    scaling = (tap_count * in_channels) ** (-0.5)
    low_weight = (scaling * master).astype(jnp.bfloat16)
    low_three = low_weight.reshape(3, 9 * in_channels, out_channels)
    rimmed = extended(local_slab, (("gz", 0),), 1)
    padded = jnp.pad(rimmed, ((0, 0), (1, 1), (1, 1), (0, 0)))
    patches, preact = forward_terms(padded, low_three, planes, plane_width)
    preact = preact + master_bias
    grad_pre = (
        spread_cotangent(cotangent[0], planes, plane_width, out_channels)
        * 0.125
        * gelu_slope(preact)
    ).astype(jnp.bfloat16)
    partial_w = scaling * weight_terms(patches, grad_pre, planes, plane_width, in_channels)
    partial_b = jnp.sum(grad_pre.astype(jnp.float32), axis=0)
    grad_rimmed = extended(
        grad_pre.reshape(planes, plane_width, plane_width, out_channels), (("gz", 0),), 1
    )
    grad_pad = jnp.pad(grad_rimmed, ((0, 0), (1, 1), (1, 1), (0, 0)))
    input_grad = input_terms(grad_pad, low_weight, planes, plane_width).astype(jnp.bfloat16)
    input_grad = input_grad.reshape(planes, plane_width, plane_width, in_channels)
    bit_count = lax.axis_size("dp").bit_length() - 1
    round_count = exponent.shape[0]
    row_total = tap_count * in_channels
    flat_w = partial_w.reshape(row_total, out_channels)
    share_w, share_b = (
        lax.psum_scatter(flat_w, "gz", scatter_dimension=0, tiled=True),
        lax.psum_scatter(partial_b, "gz", scatter_dimension=0, tiled=True),
    )
    row_share = row_total // lax.axis_size("gz")
    bias_share = out_channels // lax.axis_size("gz")
    row_offset = lax.axis_index("gz") * row_share
    bias_offset = lax.axis_index("gz") * bias_share
    own_w = lax.dynamic_slice_in_dim(
        master.reshape(row_total, out_channels), row_offset, row_share, 0
    )
    own_b = lax.dynamic_slice_in_dim(master_bias, bias_offset, bias_share, 0)
    averaged_w = own_w - learning_rate * share_w
    averaged_b = own_b - learning_rate * share_b
    for round_index in range(round_count):
        partner_w, partner_b = lax.switch(
            exponent[round_index],
            [partial(share_swap, averaged_w, averaged_b, bit) for bit in range(bit_count)],
        )
        averaged_w = 0.5 * (averaged_w + partner_w)
        averaged_b = 0.5 * (averaged_b + partner_b)
    gathered_w, mixed_b = (
        lax.all_gather(averaged_w, "gz", axis=0, tiled=True),
        lax.all_gather(averaged_b, "gz", axis=0, tiled=True),
    )
    mixed_w = gathered_w.reshape(tap_count, in_channels, out_channels)
    return (mixed_w[None], mixed_b[None], input_grad[None])


def solution(mesh):
    in_specs = (
        P("dp", "gz", None, None, None),
        P("dp", "gz", None, None, None),
        P("dp", None, None, None),
        P("dp", None),
        P(),
    )
    out_specs = (P("dp", None, None, None), P("dp", None), P("dp", "gz", None, None, None))
    return jax.shard_map(
        per_device, mesh=mesh, in_specs=in_specs, out_specs=out_specs, check_vma=False
    )
```

profile of v0, /device:TPU:0, one launch (start us, length us, event | category | flops | bytes accessed | tf_op | source)
XLA Modules:
  0.0 282.8 jit_solution(10391229836019666898)
XLA Ops:
  8.3 5.0 %collective-permute-start.24 = (bf16[1,32,32,128]{3,2,1,0:T(8,128)(2,1)S(1)}, bf16[1,32,32,128]{3,2,1,0:T(8,128)(2,1)S(1)}, u32[]{:S(2)}, u32[]{:S(2)}) collective-permute-start(bf16[1,32,32,128]{3,2,1,0:T(8,128)(2,1)S(1)} %get-tuple-element.152), channel_id=1, source_target_pairs={{0,1},{1,2},{2,3},{4,5},{5,6},{6,7},{8,9},{9,10},{10,11},{12,13},{... | collective-permute-start | bytes 786440 | tf_op jit(solution)/shard_map/ppermute | solution.py:30
  15.5 2.5 multiply_convert_fusion
  18.0 2.3 broadcast_in_dim.4
  20.3 3.7 %mul.109 = f32[2048,256]{1,0:T(8,128)} reshape(f32[2,16,2,16,2,256]{5,4,3,2,1,0:T(2,128)} %broadcast_in_dim.4) | data formatting | bytes 4194304 | tf_op jit(solution)/shard_map/mul | solution.py:130
  28.5 2.2 fusion.94
  30.7 1.6 fusion.101
  32.3 1.6 convolution_add_fusion.1
  34.0 2.7 convert_reduce_fusion
  41.1 2.1 maximum_multiply_fusion
  51.2 5.2 %collective-permute-start.26 = (bf16[1,32,32,256]{3,2,1,0:T(8,128)(2,1)}, bf16[1,32,32,256]{3,2,1,0:T(8,128)(2,1)S(1)}, u32[]{:S(2)}, u32[]{:S(2)}) collective-permute-start(bf16[1,32,32,256]{3,2,1,0:T(8,128)(2,1)} %bitcast.24), channel_id=1, source_target_pairs={{0,1},{1,2},{2,3},{4,5},{5,6},{6,7},{8,9},{9,10},{10,11},{12,13},{... | collective-permute-start | bytes 1572872 | tf_op jit(solution)/shard_map/ppermute | solution.py:30
  58.3 40.2 %all-reduce.3 = f32[256]{0:T(256)S(1)} all-reduce(f32[256]{0:T(256)S(1)} %get-tuple-element.160), channel_id=3, replica_groups=mesh['dp'=8,'gz'=4] {'gz'}, use_global_device_ids=true, to_apply=%region_2.3.clone | all-reduce | flops 256 | bytes 2048
  99.4 2.4 select_maximum_fusion
  101.8 9.2 %fusion.95 = (bf16[2,32,32,256]{3,2,1,0:T(8,128)(2,1)}, bf16[2,32,32,256]{3,2,1,0:T(8,128)(2,1)}, bf16[2,32,32,256]{3,2,1,0:T(8,128)(2,1)}, bf16[2,32,32,256]{3,...) fusion(bf16[4,34,34,256]{3,2,1,0:T(8,128)(2,1)S(1)} %select_max, ...), kind=kLoop, calls=%fused_computation.174 | loop fusion | bytes 39845888 | tf_op jit(solution)/shard_map/slice | solution.py:83
  111.0 12.6 %reduce-scatter.2.cloned.1.call-done = f32[864,256]{1,0:T(8,128)} async-done(((f32[3456,256]{1,0:T(8,128)}), f32[864,256]{1,0:T(8,128)}) %reduce-scatter.2.cloned.1.call-update) | async-done | bytes 884752 | tf_op jit(solution)/shard_map/reduce_scatter | solution.py:147
  123.6 1.5 multiply_subtract_fusion
  126.0 2.6 conditional.4
  126.5 2.0 collective-permute-done.1
  128.6 1.6 add_multiply_fusion.3
  131.1 21.9 %conditional.5 = (f32[864,256]{1,0:T(8,128)}, f32[64]{0:T(128)}) conditional(s32[]{:T(128)} %bitcast.18, (f32[864,256]{1,0:T(8,128)S(1)}, f32[64]{0:T(128)S(1)}) %tuple.57, (f32[864,256]{1,0:T(8,128)S(1)}, f32[64]{0:T(128)S(1)}) %tuple.57, (f32[864,256]{1,0:T(8,128)S(1)}, f32[64]{0:T(128)S(1)}) %tuple.57), branch_computations={%region_6.7_spmd, %region_7.8_spmd, %region_8.9_spmd} | conditional | bytes 3540064 | solution.py:161
  133.1 19.9 %collective-permute-done.11 = f32[64]{0:T(128)} collective-permute-done((f32[64]{0:T(128)S(1)}, f32[64]{0:T(128)}, u32[]{:S(2)}, u32[]{:S(2)}) %collective-permute-start.11) | collective-permute-done | bytes 288 | tf_op jit(solution)/shard_map/cond/branch_2_fun/ppermute | solution.py:20
  153.0 1.6 add_multiply_fusion.2
  155.4 21.0 %conditional.6 = (f32[864,256]{1,0:T(8,128)}, f32[64]{0:T(128)}) conditional(s32[]{:T(128)} %bitcast.19, (f32[864,256]{1,0:T(8,128)S(1)}, f32[64]{0:T(128)S(1)}) %tuple.58, (f32[864,256]{1,0:T(8,128)S(1)}, f32[64]{0:T(128)S(1)}) %tuple.58, (f32[864,256]{1,0:T(8,128)S(1)}, f32[64]{0:T(128)S(1)}) %tuple.58), branch_computations={%region_9.10_spmd, %region_10.11_spmd, %region_11.12_spmd} | conditional | bytes 3540064 | solution.py:161
  157.5 18.9 %collective-permute-done.15 = f32[64]{0:T(128)} collective-permute-done((f32[64]{0:T(128)S(1)}, f32[64]{0:T(128)}, u32[]{:S(2)}, u32[]{:S(2)}) %collective-permute-start.15) | collective-permute-done | bytes 288 | tf_op jit(solution)/shard_map/cond/branch_1_fun/ppermute | solution.py:20
  176.4 1.6 add_multiply_fusion.1
  178.9 20.0 %conditional.7 = (f32[864,256]{1,0:T(8,128)}, f32[64]{0:T(128)}) conditional(s32[]{:T(128)} %bitcast.20, (f32[864,256]{1,0:T(8,128)S(1)}, f32[64]{0:T(128)S(1)}) %tuple.59, (f32[864,256]{1,0:T(8,128)S(1)}, f32[64]{0:T(128)S(1)}) %tuple.59, (f32[864,256]{1,0:T(8,128)S(1)}, f32[64]{0:T(128)S(1)}) %tuple.59), branch_computations={%region_12.13_spmd, %region_13.14_spmd, %region_14.15_spmd} | conditional | bytes 3540064 | solution.py:161
  180.9 18.0 %collective-permute-done.23 = f32[64]{0:T(128)} collective-permute-done((f32[64]{0:T(128)S(1)}, f32[64]{0:T(128)}, u32[]{:S(2)}, u32[]{:S(2)}) %collective-permute-start.23) | collective-permute-done | bytes 288 | tf_op jit(solution)/shard_map/cond/branch_2_fun/ppermute | solution.py:20
  198.9 2.5 add_multiply_fusion
  201.4 2.8 %fusion.7 = f32[2048,128]{1,0:T(8,128)S(1)} fusion(bf16[2048,256]{1,0:T(8,128)(2,1)} %bitcast.197, bf16[2048,256]{1,0:T(8,128)(2,1)} %copy-done, bf16[2048,256]{1,0:T(8,128)(2,1)} %bitcast.198, bf16[256,128]{0,1:T(8,128)(2,1)} %get-tuple-element.130, bf16[256,128]{0,1:T(8,128)(2,1)} %get-tuple-element.131, bf16[256,128]{0,1:T(8,128)(2,1)} %get-tuple-element.132), kind=kOutput, calls=%fused_computation.18 | convolution fusion | flops 412680192 | bytes 4390912 | tf_op jit(solution)/shard_map/dot_general | solution.py:97
  222.0 1.8 fusion.20
  224.5 11.9 %all-reduce.2 = f32[256]{0:T(256)} all-reduce(f32[256]{0:T(256)S(1)} %multiply_dynamic-update-slice_fusion), channel_id=1, replica_groups=mesh['dp'=8,'gz'=4] {'gz'}, use_global_device_ids=true, to_apply=%add.2 | all-reduce | flops 256 | bytes 2048
  236.4 35.4 %all-gather.2.cloned.1.call-done = f32[3456,256]{1,0:T(8,128)} async-done(((f32[864,256]{1,0:T(8,128)}), f32[3456,256]{1,0:T(8,128)}) %all-gather.2.cloned.1.call-update) | async-done | bytes 3538960 | tf_op jit(solution)/shard_map/all_gather | solution.py:168
  271.8 4.2 %copy.42 = f32[1,27,128,256]{3,2,1,0:T(8,128)} copy(f32[1,27,128,256]{3,2,1,0:T(8,128)} %bitcast.194) | data formatting | bytes 7077888
  (163 shorter events, 47.3 us)
Async XLA Ops:
  7.2 116.4 %reduce-scatter.2.cloned.1.call-start = ((), (), s32[]{:S(2)}) async-start(), calls=%async_computation.1 | async-start | bytes 4423680 | tf_op jit(solution)/shard_map/reduce_scatter | solution.py:147
  8.3 15.9 %collective-permute-start.24 = (bf16[1,32,32,128]{3,2,1,0:T(8,128)(2,1)S(1)}, bf16[1,32,32,128]{3,2,1,0:T(8,128)(2,1)S(1)}, u32[]{:S(2)}, u32[]{:S(2)}) collective-permute-start(bf16[1,32,32,128]{3,2,1,0:T(8,128)(2,1)S(1)} %get-tuple-element.152), channel_id=1, source_target_pairs={{0,1},{1,2},{2,3},{4,5},{5,6},{6,7},{8,9},{9,10},{10,11},{12,13},{... | collective-permute-start | bytes 786440 | tf_op jit(solution)/shard_map/ppermute | solution.py:30
  13.3 10.9 %collective-permute-start.25 = (bf16[1,32,32,128]{3,2,1,0:T(8,128)(2,1)S(1)}, bf16[1,32,32,128]{3,2,1,0:T(8,128)(2,1)S(1)}, u32[]{:S(2)}, u32[]{:S(2)}) collective-permute-start(bf16[1,32,32,128]{3,2,1,0:T(8,128)(2,1)S(1)} %get-tuple-element.153), channel_id=1, source_target_pairs={{1,0},{2,1},{3,2},{5,4},{6,5},{7,6},{9,8},{10,9},{11,10},{13,12},{... | collective-permute-start | bytes 786440 | tf_op jit(solution)/shard_map/ppermute | solution.py:31
  20.3 3.9 %copy-start.2 = (bf16[1,2,32,32,128]{4,3,2,1,0:T(8,128)(2,1)S(1)}, bf16[1,2,32,32,128]{4,3,2,1,0:T(8,128)(2,1)}, u32[]{:S(2)}) copy-start(bf16[1,2,32,32,128]{4,3,2,1,0:T(8,128)(2,1)} %param.17) | copy-start | bytes 1572868
  32.3 1.7 copy-start.26
  32.3 1.7 copy-start.50
  36.7 12.2 %copy-start = (bf16[2048,256]{1,0:T(8,128)(2,1)}, bf16[2048,256]{1,0:T(8,128)(2,1)S(1)}, u32[]{:S(2)}) copy-start(bf16[2048,256]{1,0:T(8,128)(2,1)S(1)} %get-tuple-element.161) | copy-start | bytes 3145732
  43.2 3.8 %copy-start.49 = (u32[32]{0:T(128)S(1)}, u32[32]{0:T(128)}, u32[]{:S(2)}) copy-start(u32[32]{0:T(128)} %constant.56) | copy-start | bytes 388
  43.2 228.6 %all-gather.2.cloned.1.call-start = ((), (), s32[]{:S(2)}) async-start(), calls=%async_computation.2 | async-start | bytes 4423680 | tf_op jit(solution)/shard_map/all_gather | solution.py:168
  49.9 48.6 %collective-permute-start.27 = (bf16[1,32,32,256]{3,2,1,0:T(8,128)(2,1)}, bf16[1,32,32,256]{3,2,1,0:T(8,128)(2,1)S(1)}, u32[]{:S(2)}, u32[]{:S(2)}) collective-permute-start(bf16[1,32,32,256]{3,2,1,0:T(8,128)(2,1)} %bitcast.26), channel_id=1, source_target_pairs={{1,0},{2,1},{3,2},{5,4},{6,5},{7,6},{9,8},{10,9},{11,10},{13,12},{... | collective-permute-start | bytes 1572872 | tf_op jit(solution)/shard_map/ppermute | solution.py:31
  51.2 47.3 %collective-permute-start.26 = (bf16[1,32,32,256]{3,2,1,0:T(8,128)(2,1)}, bf16[1,32,32,256]{3,2,1,0:T(8,128)(2,1)S(1)}, u32[]{:S(2)}, u32[]{:S(2)}) collective-permute-start(bf16[1,32,32,256]{3,2,1,0:T(8,128)(2,1)} %bitcast.24), channel_id=1, source_target_pairs={{0,1},{1,2},{2,3},{4,5},{5,6},{6,7},{8,9},{9,10},{10,11},{12,13},{... | collective-permute-start | bytes 1572872 | tf_op jit(solution)/shard_map/ppermute | solution.py:30
  126.0 2.6 collective-permute-start
  126.0 2.6 collective-permute-start.1
  131.1 21.9 %collective-permute-start.10 = (f32[864,256]{1,0:T(8,128)S(1)}, f32[864,256]{1,0:T(8,128)}, u32[]{:S(2)}, u32[]{:S(2)}) collective-permute-start(f32[864,256]{1,0:T(8,128)S(1)} %get-tuple-element.58), channel_id=1, source_target_pairs={{0,16},{16,0},{4,20},{20,4},{8,24},{24,8},{12,28},{28,12},{1,17},{... | collective-permute-start | bytes 2654216 | tf_op jit(solution)/shard_map/cond/branch_2_fun/ppermute | solution.py:20
  132.5 20.4 %collective-permute-start.11 = (f32[64]{0:T(128)S(1)}, f32[64]{0:T(128)}, u32[]{:S(2)}, u32[]{:S(2)}) collective-permute-start(f32[64]{0:T(128)S(1)} %get-tuple-element.59), channel_id=1, source_target_pairs={{0,16},{16,0},{4,20},{20,4},{8,24},{24,8},{12,28},{28,12},{1,17},{... | collective-permute-start | bytes 776 | tf_op jit(solution)/shard_map/cond/branch_2_fun/ppermute | solution.py:20
  155.4 21.0 %collective-permute-start.14 = (f32[864,256]{1,0:T(8,128)S(1)}, f32[864,256]{1,0:T(8,128)}, u32[]{:S(2)}, u32[]{:S(2)}) collective-permute-start(f32[864,256]{1,0:T(8,128)S(1)} %get-tuple-element.62), channel_id=1, source_target_pairs={{0,8},{8,0},{4,12},{12,4},{16,24},{24,16},{20,28},{28,20},{1,9},{9... | collective-permute-start | bytes 2654216 | tf_op jit(solution)/shard_map/cond/branch_1_fun/ppermute | solution.py:20
  156.9 19.5 %collective-permute-start.15 = (f32[64]{0:T(128)S(1)}, f32[64]{0:T(128)}, u32[]{:S(2)}, u32[]{:S(2)}) collective-permute-start(f32[64]{0:T(128)S(1)} %get-tuple-element.63), channel_id=1, source_target_pairs={{0,8},{8,0},{4,12},{12,4},{16,24},{24,16},{20,28},{28,20},{1,9},{9... | collective-permute-start | bytes 776 | tf_op jit(solution)/shard_map/cond/branch_1_fun/ppermute | solution.py:20
  178.9 20.0 %collective-permute-start.22 = (f32[864,256]{1,0:T(8,128)S(1)}, f32[864,256]{1,0:T(8,128)}, u32[]{:S(2)}, u32[]{:S(2)}) collective-permute-start(f32[864,256]{1,0:T(8,128)S(1)} %get-tuple-element.70), channel_id=1, source_target_pairs={{0,16},{16,0},{4,20},{20,4},{8,24},{24,8},{12,28},{28,12},{1,17},{... | collective-permute-start | bytes 2654216 | tf_op jit(solution)/shard_map/cond/branch_2_fun/ppermute | solution.py:20
  180.3 18.5 %collective-permute-start.23 = (f32[64]{0:T(128)S(1)}, f32[64]{0:T(128)}, u32[]{:S(2)}, u32[]{:S(2)}) collective-permute-start(f32[64]{0:T(128)S(1)} %get-tuple-element.71), channel_id=1, source_target_pairs={{0,16},{16,0},{4,20},{20,4},{8,24},{24,8},{12,28},{28,12},{1,17},{... | collective-permute-start | bytes 776 | tf_op jit(solution)/shard_map/cond/branch_2_fun/ppermute | solution.py:20
  204.2 1.8 copy-start.18
  204.2 2.1 copy-start.19
  204.2 2.3 copy-start.25
  207.5 1.7 copy-start.16
  210.1 1.7 copy-start.10
  210.1 2.1 copy-start.11
  210.1 2.4 copy-start.12
  210.2 2.8 copy-start.13
  210.2 3.1 %copy-start.14 = (bf16[2,32,32,256]{3,2,1,0:T(8,128)(2,1)S(1)}, bf16[2,32,32,256]{3,2,1,0:T(8,128)(2,1)}, u32[]{:S(2)}) copy-start(bf16[2,32,32,256]{3,2,1,0:T(8,128)(2,1)} %get-tuple-element.103) | copy-start | bytes 3145732
  215.2 1.8 copy-start.5
  215.2 2.2 copy-start.6
  215.2 2.5 copy-start.7
  215.2 2.8 copy-start.8
  (33 other events, 33.2 us)
Sparse Core Ops, SparseCore 0:
  43.3 80.1 reduce-scatter.1
  201.5 70.2 all-gather.1
where the time goes:
time: 284 us; the launch traced here: 283 us
  waiting for transfers between devices  107 us (38%)
  blocking collectives  52.2 us (18%)
  local copies, waits for them, and re-layouts  42.1 us (15%)
  other arithmetic  21.9 us (8%)
  matrix products  21.8 us (8%)
  starting transfers between devices  19.4 us (7%)
  between operations  18.6 us (7%)
    ppermute x8, waiting for transfers between devices, from_partner(): return lax.ppermute(block, axis, route)  58.8 us
    unnamed x2, blocking collectives  52.2 us
    all_gather x1, waiting for transfers between devices, per_device(): lax.all_gather(averaged_w, 'gz', axis=0, tiled=True)  35.4 us
    unnamed x112, local copies, waits for them, and re-layouts  18.5 us
    reduce_scatter x1, waiting for transfers between devices, per_device(): lax.psum_scatter(flat_w, 'gz', scatter_dimension=0, tiled=True)  12.6 us
    dot_general x9, matrix products, input_terms(): jnp.dot(pieces.reshape(cell_count, -1), kernel_block, preferred_element_t...  11.6 us
    ppermute x2, starting transfers between devices, extended(): before = lax.ppermute(last, axis, up)  10.2 us
    slice x2, local copies, waits for them, and re-layouts, input_terms(): grad_pad[2 - depth_off:2 - depth_off + planes, 2 - row_off:2 - row_off +...  10 us
  transfers between devices with their start and end apart: 14, of which 6 were waited for; matrix products, arithmetic and copies ran while one was open for 14% of the time, Pallas kernels for 0%

commit v1 on v0

v1 whole, which is shorter than its diff:
```python
from functools import partial
import math

import jax
import jax.numpy as jnp
from jax import lax
from jax.experimental import pallas as pl
from jax.experimental.pallas import tpu as pltpu
from jax.sharding import PartitionSpec as P

learning_rate = 0.5
cubic = 0.044715
f32 = jnp.float32
bf16 = jnp.bfloat16
VMEM = pl.BlockSpec(memory_space=pltpu.VMEM)
SMEM = pl.BlockSpec(memory_space=pltpu.SMEM)
ANY = pl.BlockSpec(memory_space=pl.ANY)


def gelu_slope(values):
    factor = math.sqrt(2.0 / math.pi)
    inner_arg = factor * (values + cubic * values * values * values)
    tangent = jnp.tanh(inner_arg)
    return 0.5 * (1.0 + tangent) + 0.5 * values * (1.0 - tangent * tangent) * factor * (
        1.0 + 3.0 * cubic * values * values
    )


def col_shifts(flat, width):
    cells = flat.shape[0]
    wide = flat.astype(f32)
    col = lax.broadcasted_iota(jnp.int32, flat.shape, 0) % width
    before = jnp.where(col == 0, 0.0, pltpu.roll(wide, 1, 0)).astype(flat.dtype)
    after = jnp.where(col == width - 1, 0.0, pltpu.roll(wide, cells - 1, 0)).astype(flat.dtype)
    return before, after


def fill_shifted(dst, plane, left, mid, right):
    rows, width = dst.shape[1] - 2, dst.shape[2]
    chans = mid.shape[1]
    blank = jnp.zeros((1, width, 3 * chans), dst.dtype)
    dst[plane, 0:1] = blank
    dst[plane, rows + 1 : rows + 2] = blank
    for c, part in enumerate((left, mid, right)):
        dst[plane, 1 : rows + 1, :, c * chans : (c + 1) * chans] = part.reshape(rows, width, chans)


def row_dot(src, plane, row, step, weights, flip=False):
    width = src.shape[2]
    parts = [
        src[plane, pl.ds(row + (2 - b if flip else b), step)].reshape(step * width, src.shape[3])
        for b in range(3)
    ]
    lhs = jnp.concatenate(parts, axis=1)
    dims = (((1,), (0,)), ((), ()))
    return lax.dot_general(lhs, weights, dims, preferred_element_type=f32)


def prep_kernel(scaling, step, vol, weight, cot, xs, low, pre, cup):
    planes, rows, width, chans = vol.shape
    half = cot.shape[0]
    for plane in range(planes):
        flat = vol[plane].reshape(rows * width, chans)
        before, after = col_shifts(flat, width)
        fill_shifted(xs, plane, before, flat, after)
    low[...] = (scaling * weight[...]).astype(bf16)
    small = cot.shape[1] * half
    tall = half * width
    row = lax.broadcasted_iota(jnp.int32, (tall, small), 0)
    col = lax.broadcasted_iota(jnp.int32, (tall, small), 1)
    pick = (row // width) * cot.shape[1] + (row % width) // 2 == col
    wide = lax.dot_general(
        pick.astype(f32).astype(bf16), cot[...].reshape(small, cot.shape[2]),
        (((1,), (0,)), ((), ())), preferred_element_type=f32,
    )
    cup[...] = wide.reshape(half, width, cot.shape[2]).astype(bf16)
    taps, _, outs = low.shape
    for plane in range(planes):
        for block in range(rows // step):
            total = None
            for a in range(3):
                source = plane + a - 1
                if source < 0 or source >= planes:
                    continue
                part = row_dot(
                    xs, source, block * step, step, low[9 * a : 9 * a + 9].reshape(9 * chans, outs)
                )
                total = part if total is None else total + part
            pre[plane, pl.ds(block * step, step)] = total.reshape(step, width, outs)


def main_kernel(
    scaling, gz, step, split, ids, lo, hi, xs, low, pre, cup, bias, weight,
    send_a, top_a, keep_a, send_b, top_b, keep_b, grad, xh, tiles,
):
    planes, rows, width, outs = pre.shape
    chans = weight.shape[1]
    for side, ref in enumerate((lo, hi)):
        flat = ref[...].reshape(rows * width, chans)
        flat = jnp.where(ids[2 + side] == 0, jnp.zeros_like(flat), flat)
        before, after = col_shifts(flat, width)
        fill_shifted(xh, side, before, flat, after)
    sums = jnp.zeros((1, outs), f32)
    for plane in range(planes):
        for block in range(rows // step):
            span = pl.ds(block * step, step)
            total = pre[plane, span].reshape(step * width, outs) + bias[...]
            if plane == 0:
                total += row_dot(xh, 0, block * step, step, low[0:9].reshape(9 * chans, outs))
            if plane == planes - 1:
                total += row_dot(xh, 1, block * step, step, low[18:27].reshape(9 * chans, outs))
            slope = gelu_slope(total).reshape(step, width, outs)
            got = []
            for pair in range(step // 2):
                up = cup[(plane // 2) * (rows // 2) + block * (step // 2) + pair].astype(f32) * 0.125
                for inner in range(2):
                    got.append((up * slope[2 * pair + inner]).astype(bf16)[None])
            block_grad = jnp.concatenate(got, axis=0)
            grad[plane, span] = block_grad
            flat = block_grad.reshape(step * width, outs).astype(f32)
            sums += jnp.sum(flat, axis=0, keepdims=True)
    blocks, _, high, lanes = tiles.shape
    halves = outs // lanes

    def emit(tile, slot, which):
        send, top, keep = which
        for index in range(blocks):
            i, h = divmod(index, halves)
            tiles[index, 0] = tile[i * high : (i + 1) * high, h * lanes : (h + 1) * lanes].astype(bf16)
        me = ids[0] if send is send_a else ids[1]
        for rel in range(blocks):
            value = tiles[lax.bitwise_xor(me, rel), 0]
            if rel >= blocks // 2:
                send[rel - blocks // 2, slot] = value
            elif rel >= blocks // 4:
                top[rel - blocks // 4, slot] = value
            else:
                keep[rel, slot] = value

    first = (send_a, top_a, keep_a)
    second = (send_b, top_b, keep_b)
    for group in range(9):
        a, b = divmod(group, 3)
        total = None
        for plane in range(planes):
            source = plane + a - 1
            if source < 0:
                lhs = xh[0, b : b + rows]
            elif source >= planes:
                lhs = xh[1, b : b + rows]
            else:
                lhs = xs[source, b : b + rows]
            part = lax.dot_general(
                lhs.reshape(rows * width, 3 * chans), grad[plane].reshape(rows * width, outs),
                (((0,), (0,)), ((), ())), preferred_element_type=f32,
            )
            total = part if total is None else total + part
        for c in range(3):
            tap = 3 * group + c
            tile = (1.0 / gz) * weight[tap] - (learning_rate * scaling) * total[c * chans : (c + 1) * chans]
            if tap < split:
                emit(tile, tap, first)
            else:
                emit(tile, tap - split, second)
    tile = (1.0 / gz) * bias[...] - learning_rate * sums
    emit(jnp.broadcast_to(tile, (chans, outs)), weight.shape[0] - split, second)


def input_kernel(step, grad, low, own, below, above, gs, acc, wt):
    planes, rows, width, outs = grad.shape
    chans = low.shape[1]
    for plane in range(planes):
        flat = grad[plane].reshape(rows * width, outs)
        before, after = col_shifts(flat, width)
        fill_shifted(gs, plane, after, flat, before)
    for tap in range(low.shape[0]):
        a, b, c = tap // 9, tap // 3 % 3, tap % 3
        wt[(3 * b + c) * outs : (3 * b + c + 1) * outs, a * chans : (a + 1) * chans] = low[tap].T
    for plane in range(planes):
        for block in range(rows // step):
            span = pl.ds(block * step, step)
            got = row_dot(gs, plane, block * step, step, wt[...], flip=True)
            for a in range(3):
                target = plane + a
                part = got[:, a * chans : (a + 1) * chans].reshape(step, width, chans)
                if target == 0:
                    below[span] = part.astype(bf16)
                elif target == planes + 1:
                    above[span] = part.astype(bf16)
                elif plane == max(0, target - 2):
                    acc[target - 1, span] = part
                else:
                    acc[target - 1, span] = acc[target - 1, span] + part
    own[...] = acc[...]


def final_kernel(split, count, ids, *refs):
    pieces_a, pieces_b = refs[:count], refs[count : 2 * count]
    new_w, new_b, buf, sem = refs[2 * count :]
    taps, chans, outs = buf.shape
    starts = [0]
    for piece in pieces_a:
        starts.append(starts[-1] + piece.shape[0])
    blocks = starts[-1]
    high, lanes = pieces_a[0].shape[2:]
    halves = outs // lanes
    copies = []
    for which, (pieces, begin, end) in enumerate(((pieces_a, 0, split), (pieces_b, split, taps))):
        for k, piece in enumerate(pieces):
            for j in range(piece.shape[0]):
                place = lax.bitwise_xor(ids[which], starts[k] + j)
                i, h = place // halves, place % halves
                buf[
                    begin:end,
                    pl.ds(pl.multiple_of(i * high, high), high),
                    pl.ds(pl.multiple_of(h * lanes, lanes), lanes),
                ] = piece[j, 0 : end - begin].astype(f32)
                if which == 1:
                    @pl.when(i == 0)
                    def _():
                        new_b[:, pl.ds(pl.multiple_of(h * lanes, lanes), lanes)] = (
                            piece[j, end - begin, 0:1].astype(f32)
                        )
        copy = pltpu.make_async_copy(buf.at[begin:end], new_w.at[begin:end], sem.at[which])
        copy.start()
        copies.append(copy)
    for copy in copies:
        copy.wait()


def swap(block, axis, mask):
    count = lax.axis_size(axis)
    return lax.ppermute(block, axis, [(i, i ^ mask) for i in range(count)])


def total_of(left, right):
    return (left.astype(f32) + right.astype(f32)).astype(bf16)


def per_device(volume, cotangent, weight, bias, exponent):
    vol, cot, master = volume[0], cotangent[0], weight[0]
    planes, rows, width, chans = vol.shape
    taps, _, outs = master.shape
    scaling = (taps * chans) ** (-0.5)
    gz, dp = lax.axis_size("gz"), lax.axis_size("dp")
    gz_bits, dp_bits = gz.bit_length() - 1, dp.bit_length() - 1
    zi, di = lax.axis_index("gz"), lax.axis_index("dp")
    split = 15
    step = 8
    lanes = 128
    blocks = 4 * gz
    halves = outs // lanes
    high = chans * halves // blocks
    slots = (split, taps - split + 1)
    low_bit, high_bit = di & 1, di >> (dp_bits - 1)
    path_a = [("dp", 1), ("dp", dp // 2)] + [("gz", 1 << k) for k in range(gz_bits)]
    path_b = [("dp", 1), ("gz", 1), ("dp", dp // 2)] + [("gz", 1 << k) for k in range(1, gz_bits)]

    def number(path):
        value = 0
        for axis, mask in path:
            bit = ((di if axis == "dp" else zi) & mask) // mask
            value = value * 2 + bit
        return value.astype(jnp.int32)

    me_a, me_b = number(path_a), number(path_b)
    ids = jnp.stack([me_a, me_b, (zi > 0).astype(jnp.int32), (zi < gz - 1).astype(jnp.int32)])

    even = (zi & 1) == 0
    inner = []
    for low_z in range(1, gz - 1, 2):
        inner += [(low_z, low_z + 1), (low_z + 1, low_z)]

    def trade(first, last):
        paired = swap(jnp.where(even, last, first), "gz", 1)
        other = lax.ppermute(jnp.where(even, first, last), "gz", inner)
        return jnp.where(even, other, paired), jnp.where(even, paired, other)

    below, above = trade(vol[0], vol[planes - 1])
    sds = jax.ShapeDtypeStruct
    params = pltpu.CompilerParams(vmem_limit_bytes=60 * 1024 * 1024)
    xs, low, pre, cup = pl.pallas_call(
        partial(prep_kernel, scaling, step),
        out_shape=(
            sds((planes, rows + 2, width, 3 * chans), bf16),
            sds((taps, chans, outs), bf16),
            sds((planes, rows, width, outs), f32),
            sds((planes // 2 * rows // 2, width, outs), bf16),
        ),
        in_specs=[VMEM] * 3, out_specs=(VMEM,) * 4, compiler_params=params, name="prep",
    )(vol, master, cot.reshape(planes // 2 * rows // 2, width // 2, outs))

    def parts(slot):
        return tuple(
            sds((n, slot, high, lanes), bf16) for n in (blocks // 2, blocks // 4, blocks // 4)
        )

    got = pl.pallas_call(
        partial(main_kernel, scaling, gz, step, split),
        out_shape=parts(slots[0]) + parts(slots[1]) + (sds((planes, rows, width, outs), bf16),),
        in_specs=[SMEM] + [VMEM] * 8, out_specs=(VMEM,) * 7,
        scratch_shapes=[
            pltpu.VMEM((2, rows + 2, width, 3 * chans), bf16),
            pltpu.VMEM((blocks, 1, high, lanes), bf16),
        ],
        compiler_params=params, name="main",
    )(ids, below, above, xs, low, pre, cup, bias, master)
    triple_a, triple_b, grad = got[:3], got[3:6], got[6]

    hits = [jnp.any(exponent == k) for k in range(dp_bits)]

    def input_part():
        own, to_below, to_above = pl.pallas_call(
            partial(input_kernel, step),
            out_shape=(
                sds((planes, rows, width, chans), f32),
                sds((rows, width, chans), bf16),
                sds((rows, width, chans), bf16),
            ),
            in_specs=[VMEM] * 2, out_specs=(VMEM,) * 3,
            scratch_shapes=[
                pltpu.VMEM((planes, rows + 2, width, 3 * outs), bf16),
                pltpu.VMEM((planes, rows, width, chans), f32),
                pltpu.VMEM((9 * outs, 3 * chans), bf16),
            ],
            compiler_params=params, name="input_grad",
        )(grad, low)
        from_below, from_above = trade(to_below, to_above)
        from_below = jnp.where(zi > 0, from_below, jnp.zeros_like(from_below))
        from_above = jnp.where(zi < gz - 1, from_above, jnp.zeros_like(from_above))
        bottom = (own[0] + from_below.astype(f32)).astype(bf16)
        top = (own[planes - 1] + from_above.astype(f32)).astype(bf16)
        mid = own[1 : planes - 1].astype(bf16)
        return jnp.concatenate([bottom[None], mid, top[None]], axis=0)

    def finish(pieces_a, pieces_b):
        count = len(pieces_a)
        return pl.pallas_call(
            partial(final_kernel, split, count),
            out_shape=(sds((taps, chans, outs), f32), sds((1, outs), f32)),
            in_specs=[SMEM] + [VMEM] * (2 * count), out_specs=(ANY, VMEM),
            scratch_shapes=[pltpu.VMEM((taps, chans, outs), f32), pltpu.SemaphoreType.DMA((2,))],
            compiler_params=params, name="final",
        )(ids, *pieces_a, *pieces_b)

    def averaged(value, middle, scale):
        value = scale * value
        for k in middle:
            other = swap(value.astype(bf16), "dp", 1 << k)
            value = jnp.where(hits[k], 0.5 * (value + other.astype(f32)), value)
        return value

    def paired_path():
        grads = input_part()
        state = []
        for triple, path in ((triple_a, path_a), (triple_b, path_b)):
            send, top, keep = triple
            state.append([send, top, keep])
        after = []
        for send, top, keep in state:
            other = swap(send, "dp", 1)
            after.append((total_of(top, other[blocks // 4 :]), total_of(keep, other[: blocks // 4])))
        width_now = blocks // 4
        held = after
        for level in range(1, len(path_a)):
            nexts = []
            for (send, keep), path in zip(held, (path_a, path_b)):
                other = swap(send, *path[level])
                half = width_now // 2
                if half:
                    nexts.append((total_of(keep[half:], other[half:]), total_of(keep[:half], other[:half])))
                else:
                    nexts.append(keep.astype(f32) + other.astype(f32))
            held, width_now = nexts, width_now // 2
        own = []
        for value in held:
            own.append(averaged(value, range(1, dp_bits - 1), 0.25).astype(bf16))
        gathered = [[value] for value in own]
        for level in range(len(path_a) - 1, 0, -1):
            for pieces, path in zip(gathered, (path_a, path_b)):
                block = pieces[0] if len(pieces) == 1 else jnp.concatenate(pieces, axis=0)
                pieces.append(swap(block, *path[level]))
        whole = []
        for pieces in gathered:
            whole.append(pieces + [swap(piece, "dp", 1) for piece in pieces])
        return finish(*whole) + (grads,)

    def general_path():
        grads = input_part()
        whole = []
        for triple, path in ((triple_a, path_a), (triple_b, path_b)):
            send, top, keep = triple
            value = jnp.concatenate([keep, top, send], axis=0)
            value = value.reshape((2,) * len(path) + value.shape[1:])
            for level, (axis, mask) in enumerate(path):
                if axis == "gz":
                    mine = lax.slice_in_dim(value, 0, 1, axis=level)
                    theirs = lax.slice_in_dim(value, 1, 2, axis=level)
                    value = total_of(mine, swap(theirs, axis, mask))
            value = value.astype(f32)
            for k in range(dp_bits):
                other = swap(value.astype(bf16), "dp", 1 << k).astype(f32)
                if ("dp", 1 << k) in path:
                    other = jnp.flip(other, axis=path.index(("dp", 1 << k)))
                value = jnp.where(hits[k], 0.5 * (value + other), value)
            value = value.astype(bf16)
            for level, (axis, mask) in reversed(list(enumerate(path))):
                if axis == "gz":
                    value = jnp.concatenate([value, swap(value, axis, mask)], axis=level)
            value = value.reshape((blocks,) + value.shape[len(path) :])
            sizes = [1] + [1 << k for k in range(len(path))]
            pieces, begin = [], 0
            for size in sizes:
                pieces.append(value[begin : begin + size])
                begin += size
            half = pieces[:-1]
            other_half, begin = [], 0
            for piece in half:
                other_half.append(pieces[-1][begin : begin + piece.shape[0]])
                begin += piece.shape[0]
            whole.append(half + other_half)
        return finish(*whole) + (grads,)

    both = jnp.logical_and(hits[0], hits[dp_bits - 1])
    new_w, new_b, grads = lax.cond(both, paired_path, general_path)
    return new_w[None], new_b, grads[None]


def solution(mesh):
    in_specs = (
        P("dp", "gz", None, None, None),
        P("dp", "gz", None, None, None),
        P("dp", None, None, None),
        P("dp", None),
        P(),
    )
    out_specs = (P("dp", None, None, None), P("dp", None), P("dp", "gz", None, None, None))
    return jax.shard_map(
        per_device, mesh=mesh, in_specs=in_specs, out_specs=out_specs, check_vma=False
    )
```

time: 284 us -> 90.9 us (0.32)
  waiting for transfers between devices: 107 us -> 16.8 us
  blocking collectives: 52.2 us -> 0 us
  local copies, waits for them, and re-layouts: 42.1 us -> 1.51 us
  Pallas kernels: 0 us -> 27.6 us
  matrix products: 21.8 us -> 0 us
  between operations: 18.6 us -> 1.91 us
  starting transfers between devices: 19.4 us -> 34.9 us
  other arithmetic: 21.9 us -> 7.7 us
    unnamed x2 -> x0, blocking collectives: 52.2 us -> none
    ppermute x12 -> x28, waiting for transfers between devices: 58.8 us -> 16.8 us  [the longest x26 16.8 us: swap(): return lax.ppermute(block, axis, [(i, i ^ mask) for i in range(count)])]
    all_gather x1 -> x0, waiting for transfers between devices: 35.4 us -> none  [per_device(): lax.all_gather(averaged_w, 'gz', axis=0, tiled=True)]
    pallas_call x0 -> x4, Pallas kernels: none -> 27.6 us  [the longest x1 10.9 us: per_device(): pl.pallas_call(partial(main_kernel, scaling, gz, step, split), out_shape=...]
    dot_general x15 -> x0, matrix products: 21.8 us -> none  [the longest x9 11.6 us: input_terms(): jnp.dot(pieces.reshape(cell_count, -1), kernel_block, preferred_element_t...]
    unnamed x112 -> x4, local copies, waits for them, and re-layouts: 18.5 us -> 0.78 us
    ppermute x12 -> x28, starting transfers between devices: 19.3 us -> 34.9 us  [the longest x26 33.5 us: swap(): return lax.ppermute(block, axis, [(i, i ^ mask) for i in range(count)])]
    slice x7 -> x0, local copies, waits for them, and re-layouts: 15.1 us -> none  [the longest x2 10 us: input_terms(): grad_pad[2 - depth_off:2 - depth_off + planes, 2 - row_off:2 - row_off +...]
  transfers between devices with their start and end apart: 14 -> 28, of which waited for: 6 -> 11; matrix products, arithmetic and copies ran while one was open for 14% -> 6% of each run, Pallas kernels for 0% -> 15%
where the time goes in v1:
time: 90.9 us; the launch traced here: 90.6 us
  starting transfers between devices  34.9 us (38%)
  Pallas kernels  27.6 us (30%)
  waiting for transfers between devices  16.8 us (18%)
  other arithmetic  7.7 us (8%)
  between operations  1.91 us (2%)
  local copies, waits for them, and re-layouts  1.51 us (2%)
    ppermute x26, starting transfers between devices, swap(): return lax.ppermute(block, axis, [(i, i ^ mask) for i in range(count)])  33.5 us
    ppermute x26, waiting for transfers between devices, swap(): return lax.ppermute(block, axis, [(i, i ^ mask) for i in range(count)])  16.8 us
    pallas_call x1, Pallas kernels, per_device(): pl.pallas_call(partial(main_kernel, scaling, gz, step, split), out_shape=...  10.9 us
    pallas_call x1, Pallas kernels, per_device(): pl.pallas_call(partial(prep_kernel, scaling, step), out_shape=(sds((plane...  6.93 us
    pallas_call x1, Pallas kernels, input_part(): pl.pallas_call(partial(input_kernel, step), out_shape=(sds((planes, rows,...  6.23 us
    pallas_call x1, Pallas kernels, finish(): pl.pallas_call(partial(final_kernel, split, count), out_shape=(sds((taps,...  3.49 us
    convert_element_type x6, other arithmetic, total_of(): return (left.astype(f32) + right.astype(f32)).astype(bf16)  2.56 us
  transfers between devices with their start and end apart: 28, of which 11 were waited for; matrix products, arithmetic and copies ran while one was open for 6% of the time, Pallas kernels for 15%

profile of v1, /device:TPU:0, one launch (start us, length us, event | category | flops | bytes accessed | tf_op | source)
XLA Modules:
  0.0 90.6 jit_solution(1418933654325747386)
XLA Ops:
  0.6 1.1 %select_bitcast_fusion = (bf16[32,32,128]{2,1,0:T(8,128)(2,1)S(1)}, bf16[32,32,128]{2,1,0:T(8,128)(2,1)S(1)}) fusion(pred[]{:T(512)} %eq.15, bf16[1,2,32,32,128]{4,3,2,1,0:T(8,128)(2,1)} %param.7), kind=kLoop, calls=%fused_computation.64 | loop fusion | flops 262144 | bytes 1048577 | tf_op jit(solution)/shard_map/jit(_where)/select_n | solution.py:275
  1.7 3.1 %collective-permute-start.43 = (bf16[32,32,128]{2,1,0:T(8,128)(2,1)S(1)}, bf16[32,32,128]{2,1,0:T(8,128)(2,1)S(1)}, u32[]{:S(2)}, u32[]{:S(2)}) collective-permute-start(bf16[32,32,128]{2,1,0:T(8,128)(2,1)S(1)} %get-tuple-element.153), channel_id=1, source_target_pairs={{0,1},{1,0},{2,3},{3,2},{4,5},{5,4},{6,7},{7,6},{8,9},{9,8},{10,11... | collective-permute-start | bytes 786440 | tf_op jit(solution)/shard_map/ppermute | solution.py:233
  5.5 1.4 %compare_reduce_fusion = (pred[]{:T(512)}, pred[]{:T(512)}, pred[]{:T(512)}) fusion(s32[4]{0:T(128)} %param.11), kind=kLoop, calls=%fused_computation.68 | loop fusion | flops 21 | bytes 19 | tf_op jit(solution)/shard_map/reduce_or | solution.py:310
  8.1 6.9 %prep.1 = (bf16[2,34,32,384]{3,2,1,0:T(8,128)(2,1)}, bf16[27,128,256]{2,1,0:T(8,128)(2,1)S(1)}, f32[2,32,32,256]{3,2,1,0:T(8,128)}, bf16[16,32,256]{2,1,0:T(8,128)(2,1)}) custom-call(bf16[2,32,32,128]{3,2,1,0:T(8,128)(2,1)} %bitcast.68, f32[27,128,256]{2,1,0:T(8,128)} %bitcast.56, bf16[16,16,256]{2,1,0:T(8,128)(2,1)} %bitcast.75), custom_call_target="tpu_custom_call" | custom-call | tf_op jit(solution)/shard_map/prep/pallas_call | solution.py:282
  15.1 0.8 broadcast_select_fusion.4
  15.9 10.9 %main.1 = (bf16[8,15,16,128]{3,2,1,0:T(8,128)(2,1)}, bf16[4,15,16,128]{3,2,1,0:T(8,128)(2,1)S(1)}, bf16[4,15,16,128]{3,2,1,0:T(8,128)(2,1)S(1)}, bf16[8,13,16,12...) custom-call(s32[4]{0:T(128)S(1)} %pad_add_fusion.ids, ...), custom_call_target="tpu_custom_call" | custom-call | tf_op jit(solution)/shard_map/main/pallas_call | solution.py:298
  26.9 63.0 %conditional.1 = (f32[27,128,256]{2,1,0:T(8,128)}, f32[1,256]{1,0:T(1,128)S(1)}, bf16[1,2,32,32,128]{4,3,2,1,0:T(8,128)(2,1)S(1)}) conditional(s32[]{:T(128)} %convert_element_type.247, (pred[]{:T(512)}, pred[]{:T(512)}, pred[]{:T(512)}, bf16[4,15,16,128]{3,2,1,0:T(8,128)(2,1)S(1)}, bf16[4,15,16,128]{3,2,1,0:T(8,128)(2,1)S(1)}, ...), branch_computations={%region_3.4_spmd, %region_4.5_spmd} | conditional | flops 15138818 | bytes 61408044 | solution.py:425
  27.4 6.2 %input_grad.3 = (f32[2,32,32,128]{3,2,1,0:T(8,128)}, bf16[32,32,128]{2,1,0:T(8,128)(2,1)}, bf16[32,32,128]{2,1,0:T(8,128)(2,1)}) custom-call(bf16[2,32,32,256]{3,2,1,0:T(8,128)(2,1)S(1)} %get-tuple-element.82.grad, bf16[27,128,256]{2,1,0:T(8,128)(2,1)S(1)} %get-tuple-element.83.low), custom_call_target="tpu_custom_call" | custom-call | tf_op jit(solution)/shard_map/cond/branch_1_fun/input_grad/pallas_call | solution.py:313
  33.6 1.2 %add_convert_fusion.5 = (bf16[4,15,16,128]{3,2,1,0:T(8,128)(2,1)S(1)}, bf16[4,15,16,128]{3,2,1,0:T(8,128)(2,1)S(1)}) fusion(bf16[4,15,16,128]{3,2,1,0:T(8,128)(2,1)S(1)} %get-tuple-element.74, bf16[8,15,16,128]{3,2,1,0:T(8,128)(2,1)} %collective-permute-done, bf16[4,15,16,128]{3,2,1,0:T(8,128)(2,1)S(1)} %get-tuple-element.76), kind=kLoop, calls=%fused_computation.39 | loop fusion | flops 983040 | bytes 1474560 | tf_op jit(solution)/shard_map/cond/branch_1_fun/convert_element_type | solution.py:237
  34.9 1.6 %collective-permute-start.1 = (bf16[4,15,16,128]{3,2,1,0:T(8,128)(2,1)S(1)}, bf16[4,15,16,128]{3,2,1,0:T(8,128)(2,1)S(1)}, u32[]{:S(2)}, u32[]{:S(2)}) collective-permute-start(bf16[4,15,16,128]{3,2,1,0:T(8,128)(2,1)S(1)} %get-tuple-element.146), channel_id=1, source_target_pairs={{0,16},{4,20},{8,24},{12,28},{16,0},{20,4},{24,8},{28,12},{1,17},{... | collective-permute-start | bytes 737288 | tf_op jit(solution)/shard_map/cond/branch_1_fun/ppermute | solution.py:233
  36.5 1.1 %add_convert_fusion.7 = (bf16[4,13,16,128]{3,2,1,0:T(8,128)(2,1)S(1)}, bf16[4,13,16,128]{3,2,1,0:T(8,128)(2,1)S(1)}) fusion(bf16[4,13,16,128]{3,2,1,0:T(8,128)(2,1)S(1)} %get-tuple-element.77, bf16[8,13,16,128]{3,2,1,0:T(8,128)(2,1)} %collective-permute-done.12, bf16[4,13,16,128]{3,2,1,0:T(8,128)(2,1)S(1)} %get-tuple-element.79), kind=kLoop, calls=%fused_computation.41 | loop fusion | flops 851968 | bytes 1277952 | tf_op jit(solution)/shard_map/cond/branch_1_fun/convert_element_type | solution.py:237
  37.6 4.5 %collective-permute-start.13 = (bf16[4,13,16,128]{3,2,1,0:T(8,128)(2,1)S(1)}, bf16[4,13,16,128]{3,2,1,0:T(8,128)(2,1)S(1)}, u32[]{:S(2)}, u32[]{:S(2)}) collective-permute-start(bf16[4,13,16,128]{3,2,1,0:T(8,128)(2,1)S(1)} %get-tuple-element.150), channel_id=1, source_target_pairs={{0,1},{1,0},{2,3},{3,2},{4,5},{5,4},{6,7},{7,6},{8,9},{9,8},{10,11... | collective-permute-start | bytes 638984 | tf_op jit(solution)/shard_map/cond/branch_1_fun/ppermute | solution.py:233
  42.9 4.5 %collective-permute-start.2 = (bf16[2,15,16,128]{3,2,1,0:T(8,128)(2,1)S(1)}, bf16[2,15,16,128]{3,2,1,0:T(8,128)(2,1)S(1)}, u32[]{:S(2)}, u32[]{:S(2)}) collective-permute-start(bf16[2,15,16,128]{3,2,1,0:T(8,128)(2,1)S(1)} %get-tuple-element.144), channel_id=1, source_target_pairs={{0,1},{1,0},{2,3},{3,2},{4,5},{5,4},{6,7},{7,6},{8,9},{9,8},{10,11... | collective-permute-start | bytes 368648 | tf_op jit(solution)/shard_map/cond/branch_1_fun/ppermute | solution.py:233
  47.4 1.6 %collective-permute-start.14 = (bf16[2,13,16,128]{3,2,1,0:T(8,128)(2,1)S(1)}, bf16[2,13,16,128]{3,2,1,0:T(8,128)(2,1)S(1)}, u32[]{:S(2)}, u32[]{:S(2)}) collective-permute-start(bf16[2,13,16,128]{3,2,1,0:T(8,128)(2,1)S(1)} %get-tuple-element.148), channel_id=1, source_target_pairs={{0,16},{4,20},{8,24},{12,28},{16,0},{20,4},{24,8},{28,12},{1,17},{... | collective-permute-start | bytes 319496 | tf_op jit(solution)/shard_map/cond/branch_1_fun/ppermute | solution.py:233
  49.0 1.2 %collective-permute-done.2 = bf16[2,15,16,128]{3,2,1,0:T(8,128)(2,1)S(1)} collective-permute-done((bf16[2,15,16,128]{3,2,1,0:T(8,128)(2,1)S(1)}, bf16[2,15,16,128]{3,2,1,0:T(8,128)(2,1)S(1)}, u32[]{:S(2)}, u32[]{:S(2)}) %collective-permute-start.2) | collective-permute-done | bytes 122912 | tf_op jit(solution)/shard_map/cond/branch_1_fun/ppermute | solution.py:233
  50.2 1.5 %collective-permute-start.3 = (bf16[1,15,16,128]{3,2,1,0:T(8,128)(2,1)S(1)}, bf16[1,15,16,128]{3,2,1,0:T(8,128)(2,1)S(1)}, u32[]{:S(2)}, u32[]{:S(2)}) collective-permute-start(bf16[1,15,16,128]{3,2,1,0:T(8,128)(2,1)S(1)} %add_convert_fusion.12), channel_id=1, source_target_pairs={{0,2},{1,3},{2,0},{3,1},{4,6},{5,7},{6,4},{7,5},{8,10},{9,11},{10,... | collective-permute-start | bytes 184328 | tf_op jit(solution)/shard_map/cond/branch_1_fun/ppermute | solution.py:233
  52.2 1.1 %collective-permute-start.15 = (bf16[1,13,16,128]{3,2,1,0:T(8,128)(2,1)S(1)}, bf16[1,13,16,128]{3,2,1,0:T(8,128)(2,1)S(1)}, u32[]{:S(2)}, u32[]{:S(2)}) collective-permute-start(bf16[1,13,16,128]{3,2,1,0:T(8,128)(2,1)S(1)} %add_convert_fusion.14), channel_id=1, source_target_pairs={{0,2},{1,3},{2,0},{3,1},{4,6},{5,7},{6,4},{7,5},{8,10},{9,11},{10,... | collective-permute-start | bytes 159752 | tf_op jit(solution)/shard_map/cond/branch_1_fun/ppermute | solution.py:233
  53.3 2.7 %collective-permute-done.3 = bf16[1,15,16,128]{3,2,1,0:T(8,128)(2,1)S(1)} collective-permute-done((bf16[1,15,16,128]{3,2,1,0:T(8,128)(2,1)S(1)}, bf16[1,15,16,128]{3,2,1,0:T(8,128)(2,1)S(1)}, u32[]{:S(2)}, u32[]{:S(2)}) %collective-permute-start.3) | collective-permute-done | bytes 61472 | tf_op jit(solution)/shard_map/cond/branch_1_fun/ppermute | solution.py:233
  56.0 1.6 %collective-permute-start.4 = (bf16[1,15,16,128]{3,2,1,0:T(8,128)(2,1)S(1)}, bf16[1,15,16,128]{3,2,1,0:T(8,128)(2,1)S(1)}, u32[]{:S(2)}, u32[]{:S(2)}) collective-permute-start(bf16[1,15,16,128]{3,2,1,0:T(8,128)(2,1)S(1)} %fusion.14), channel_id=1, source_target_pairs={{0,8},{4,12},{8,0},{12,4},{16,24},{20,28},{24,16},{28,20},{1,9},{5... | collective-permute-start | bytes 184328 | tf_op jit(solution)/shard_map/cond/branch_1_fun/ppermute | solution.py:233
  57.6 1.4 %collective-permute-start.16 = (bf16[1,13,16,128]{3,2,1,0:T(8,128)(2,1)S(1)}, bf16[1,13,16,128]{3,2,1,0:T(8,128)(2,1)S(1)}, u32[]{:S(2)}, u32[]{:S(2)}) collective-permute-start(bf16[1,13,16,128]{3,2,1,0:T(8,128)(2,1)S(1)} %fusion.15), channel_id=1, source_target_pairs={{0,8},{4,12},{8,0},{12,4},{16,24},{20,28},{24,16},{28,20},{1,9},{5... | collective-permute-start | bytes 159752 | tf_op jit(solution)/shard_map/cond/branch_1_fun/ppermute | solution.py:233
  59.0 1.3 %collective-permute-done.4 = bf16[1,15,16,128]{3,2,1,0:T(8,128)(2,1)S(1)} collective-permute-done((bf16[1,15,16,128]{3,2,1,0:T(8,128)(2,1)S(1)}, bf16[1,15,16,128]{3,2,1,0:T(8,128)(2,1)S(1)}, u32[]{:S(2)}, u32[]{:S(2)}) %collective-permute-start.4) | collective-permute-done | bytes 61472 | tf_op jit(solution)/shard_map/cond/branch_1_fun/ppermute | solution.py:233
  61.0 1.1 %collective-permute-start.5 = (bf16[1,15,16,128]{3,2,1,0:T(8,128)(2,1)S(1)}, bf16[1,15,16,128]{3,2,1,0:T(8,128)(2,1)S(1)}, u32[]{:S(2)}, u32[]{:S(2)}) collective-permute-start(bf16[1,15,16,128]{3,2,1,0:T(8,128)(2,1)S(1)} %select_convert_fusion.2.refs_0_), channel_id=1, source_target_pairs={{0,2},{1,3},{2,0},{3,1},{4,6},{5,7},{6,4},{7,5},{8,10},{9,11},{10,... | collective-permute-start | bytes 184328 | tf_op jit(solution)/shard_map/cond/branch_1_fun/ppermute | solution.py:233
  62.8 2.0 %collective-permute-start.17 = (bf16[1,13,16,128]{3,2,1,0:T(8,128)(2,1)S(1)}, bf16[1,13,16,128]{3,2,1,0:T(8,128)(2,1)S(1)}, u32[]{:S(2)}, u32[]{:S(2)}) collective-permute-start(bf16[1,13,16,128]{3,2,1,0:T(8,128)(2,1)S(1)} %select_convert_fusion.3.refs_8_), channel_id=1, source_target_pairs={{0,2},{1,3},{2,0},{3,1},{4,6},{5,7},{6,4},{7,5},{8,10},{9,11},{10,... | collective-permute-start | bytes 159752 | tf_op jit(solution)/shard_map/cond/branch_1_fun/ppermute | solution.py:233
  64.8 1.4 %collective-permute-done.5.refs_1_ = bf16[1,15,16,128]{3,2,1,0:T(8,128)(2,1)S(1)} collective-permute-done((bf16[1,15,16,128]{3,2,1,0:T(8,128)(2,1)S(1)}, bf16[1,15,16,128]{3,2,1,0:T(8,128)(2,1)S(1)}, u32[]{:S(2)}, u32[]{:S(2)}) %collective-permute-start.5) | collective-permute-done | bytes 61472 | tf_op jit(solution)/shard_map/cond/branch_1_fun/ppermute | solution.py:233
  66.2 1.6 %collective-permute-start.6 = (bf16[2,15,16,128]{3,2,1,0:T(8,128)(2,1)S(1)}, bf16[2,15,16,128]{3,2,1,0:T(8,128)(2,1)S(1)}, u32[]{:S(2)}, u32[]{:S(2)}) collective-permute-start(bf16[2,15,16,128]{3,2,1,0:T(8,128)(2,1)S(1)} %pad_maximum_fusion.8), channel_id=1, source_target_pairs={{0,1},{1,0},{2,3},{3,2},{4,5},{5,4},{6,7},{7,6},{8,9},{9,8},{10,11... | collective-permute-start | bytes 368648 | tf_op jit(solution)/shard_map/cond/branch_1_fun/ppermute | solution.py:233
  68.5 3.6 %collective-permute-start.25 = (bf16[32,32,128]{2,1,0:T(8,128)(2,1)S(1)}, bf16[32,32,128]{2,1,0:T(8,128)(2,1)S(1)}, u32[]{:S(2)}, u32[]{:S(2)}) collective-permute-start(bf16[32,32,128]{2,1,0:T(8,128)(2,1)S(1)} %get-tuple-element.142), channel_id=1, source_target_pairs={{0,1},{1,0},{2,3},{3,2},{4,5},{5,4},{6,7},{7,6},{8,9},{9,8},{10,11... | collective-permute-start | bytes 786440 | tf_op jit(solution)/shard_map/cond/branch_1_fun/ppermute | solution.py:233
  72.2 1.6 %collective-permute-start.18 = (bf16[2,13,16,128]{3,2,1,0:T(8,128)(2,1)S(1)}, bf16[2,13,16,128]{3,2,1,0:T(8,128)(2,1)S(1)}, u32[]{:S(2)}, u32[]{:S(2)}) collective-permute-start(bf16[2,13,16,128]{3,2,1,0:T(8,128)(2,1)S(1)} %pad_maximum_fusion.9), channel_id=1, source_target_pairs={{0,16},{4,20},{8,24},{12,28},{16,0},{20,4},{24,8},{28,12},{1,17},{... | collective-permute-start | bytes 319496 | tf_op jit(solution)/shard_map/cond/branch_1_fun/ppermute | solution.py:233
  74.4 2.6 %collective-permute-done.18.refs_10_ = bf16[2,13,16,128]{3,2,1,0:T(8,128)(2,1)S(1)} collective-permute-done((bf16[2,13,16,128]{3,2,1,0:T(8,128)(2,1)S(1)}, bf16[2,13,16,128]{3,2,1,0:T(8,128)(2,1)S(1)}, u32[]{:S(2)}, u32[]{:S(2)}) %collective-permute-start.18) | collective-permute-done | bytes 106528 | tf_op jit(solution)/shard_map/cond/branch_1_fun/ppermute | solution.py:233
  78.4 4.5 %collective-permute-done.19.refs_11_ = bf16[4,13,16,128]{3,2,1,0:T(8,128)(2,1)S(1)} collective-permute-done((bf16[4,13,16,128]{3,2,1,0:T(8,128)(2,1)S(1)}, bf16[4,13,16,128]{3,2,1,0:T(8,128)(2,1)S(1)}, u32[]{:S(2)}, u32[]{:S(2)}) %collective-permute-start.19) | collective-permute-done | bytes 213024 | tf_op jit(solution)/shard_map/cond/branch_1_fun/ppermute | solution.py:233
  84.3 0.7 collective-permute-done.9.refs_5_
  86.3 3.5 %final.3 = (f32[27,128,256]{2,1,0:T(8,128)}, f32[1,256]{1,0:T(1,128)S(1)}) custom-call(s32[4]{0:T(128)S(1)} %get-tuple-element.72.ids, bf16[1,15,16,128]{3,2,1,0:T(8,128)(2,1)} %copy-done.4, bf16[1,15,16,128]{3,2,1,0:T(8,128)(2,1)} %copy-done.6, bf16[2,15,16,128]{3,2,1,0:T(8,128)(2,1)} %copy-done.8, bf16[4,15,16,128]{3,2,1,0:T(8,128)(2,1)} %copy-done.14, ...), custom_call_target="tpu_custom_call" | custom-call | tf_op jit(solution)/shard_map/cond/branch_1_fun/final/pallas_call | solution.py:338
  89.8 0.8 copy-done.7
  (92 shorter events, 9.4 us)
Async XLA Ops:
  1.7 13.4 %collective-permute-start.43 = (bf16[32,32,128]{2,1,0:T(8,128)(2,1)S(1)}, bf16[32,32,128]{2,1,0:T(8,128)(2,1)S(1)}, u32[]{:S(2)}, u32[]{:S(2)}) collective-permute-start(bf16[32,32,128]{2,1,0:T(8,128)(2,1)S(1)} %get-tuple-element.153), channel_id=1, source_target_pairs={{0,1},{1,0},{2,3},{3,2},{4,5},{5,4},{6,7},{7,6},{8,9},{9,8},{10,11... | collective-permute-start | bytes 786440 | tf_op jit(solution)/shard_map/ppermute | solution.py:233
  4.8 10.3 %collective-permute-start.42 = (bf16[32,32,128]{2,1,0:T(8,128)(2,1)S(1)}, bf16[32,32,128]{2,1,0:T(8,128)(2,1)S(1)}, u32[]{:S(2)}, u32[]{:S(2)}) collective-permute-start(bf16[32,32,128]{2,1,0:T(8,128)(2,1)S(1)} %get-tuple-element.154), channel_id=1, source_target_pairs={{1,2},{2,1},{5,6},{6,5},{9,10},{10,9},{13,14},{14,13},{17,18},{18,... | collective-permute-start | bytes 786440 | tf_op jit(solution)/shard_map/ppermute | solution.py:276
  26.9 6.7 %collective-permute-start = (bf16[8,15,16,128]{3,2,1,0:T(8,128)(2,1)}, bf16[8,15,16,128]{3,2,1,0:T(8,128)(2,1)}, u32[]{:S(2)}, u32[]{:S(2)}) collective-permute-start(bf16[8,15,16,128]{3,2,1,0:T(8,128)(2,1)} %get-tuple-element.75), channel_id=1, source_target_pairs={{0,4},{4,0},{8,12},{12,8},{16,20},{20,16},{24,28},{28,24},{1,5},{5... | collective-permute-start | bytes 1474568 | tf_op jit(solution)/shard_map/cond/branch_1_fun/ppermute | solution.py:233
  26.9 9.6 %collective-permute-start.12 = (bf16[8,13,16,128]{3,2,1,0:T(8,128)(2,1)}, bf16[8,13,16,128]{3,2,1,0:T(8,128)(2,1)}, u32[]{:S(2)}, u32[]{:S(2)}) collective-permute-start(bf16[8,13,16,128]{3,2,1,0:T(8,128)(2,1)} %get-tuple-element.78), channel_id=1, source_target_pairs={{0,4},{4,0},{8,12},{12,8},{16,20},{20,16},{24,28},{28,24},{1,5},{5... | collective-permute-start | bytes 1277960 | tf_op jit(solution)/shard_map/cond/branch_1_fun/ppermute | solution.py:233
  33.6 34.2 %copy-start.12 = (bf16[32,32,128]{2,1,0:T(8,128)(2,1)S(1)}, bf16[32,32,128]{2,1,0:T(8,128)(2,1)}, u32[]{:S(2)}) copy-start(bf16[32,32,128]{2,1,0:T(8,128)(2,1)} %get-tuple-element.87) | copy-start | bytes 786436 | tf_op jit(solution)/shard_map/cond
  33.6 34.2 %copy-start.13 = (bf16[32,32,128]{2,1,0:T(8,128)(2,1)S(1)}, bf16[32,32,128]{2,1,0:T(8,128)(2,1)}, u32[]{:S(2)}) copy-start(bf16[32,32,128]{2,1,0:T(8,128)(2,1)} %get-tuple-element.88) | copy-start | bytes 786436 | tf_op jit(solution)/shard_map/cond
  34.9 48.5 %copy-start.2 = (f32[2,32,32,128]{3,2,1,0:T(8,128)S(1)}, f32[2,32,32,128]{3,2,1,0:T(8,128)}, u32[]{:S(2)}) copy-start(f32[2,32,32,128]{3,2,1,0:T(8,128)} %get-tuple-element.84) | copy-start | bytes 3145732 | tf_op jit(solution)/shard_map/cond
  34.9 7.9 %collective-permute-start.1 = (bf16[4,15,16,128]{3,2,1,0:T(8,128)(2,1)S(1)}, bf16[4,15,16,128]{3,2,1,0:T(8,128)(2,1)S(1)}, u32[]{:S(2)}, u32[]{:S(2)}) collective-permute-start(bf16[4,15,16,128]{3,2,1,0:T(8,128)(2,1)S(1)} %get-tuple-element.146), channel_id=1, source_target_pairs={{0,16},{4,20},{8,24},{12,28},{16,0},{20,4},{24,8},{28,12},{1,17},{... | collective-permute-start | bytes 737288 | tf_op jit(solution)/shard_map/cond/branch_1_fun/ppermute | solution.py:233
  37.6 9.7 %collective-permute-start.13 = (bf16[4,13,16,128]{3,2,1,0:T(8,128)(2,1)S(1)}, bf16[4,13,16,128]{3,2,1,0:T(8,128)(2,1)S(1)}, u32[]{:S(2)}, u32[]{:S(2)}) collective-permute-start(bf16[4,13,16,128]{3,2,1,0:T(8,128)(2,1)S(1)} %get-tuple-element.150), channel_id=1, source_target_pairs={{0,1},{1,0},{2,3},{3,2},{4,5},{5,4},{6,7},{7,6},{8,9},{9,8},{10,11... | collective-permute-start | bytes 638984 | tf_op jit(solution)/shard_map/cond/branch_1_fun/ppermute | solution.py:233
  42.9 7.3 %collective-permute-start.2 = (bf16[2,15,16,128]{3,2,1,0:T(8,128)(2,1)S(1)}, bf16[2,15,16,128]{3,2,1,0:T(8,128)(2,1)S(1)}, u32[]{:S(2)}, u32[]{:S(2)}) collective-permute-start(bf16[2,15,16,128]{3,2,1,0:T(8,128)(2,1)S(1)} %get-tuple-element.144), channel_id=1, source_target_pairs={{0,1},{1,0},{2,3},{3,2},{4,5},{5,4},{6,7},{7,6},{8,9},{9,8},{10,11... | collective-permute-start | bytes 368648 | tf_op jit(solution)/shard_map/cond/branch_1_fun/ppermute | solution.py:233
  47.4 4.8 %collective-permute-start.14 = (bf16[2,13,16,128]{3,2,1,0:T(8,128)(2,1)S(1)}, bf16[2,13,16,128]{3,2,1,0:T(8,128)(2,1)S(1)}, u32[]{:S(2)}, u32[]{:S(2)}) collective-permute-start(bf16[2,13,16,128]{3,2,1,0:T(8,128)(2,1)S(1)} %get-tuple-element.148), channel_id=1, source_target_pairs={{0,16},{4,20},{8,24},{12,28},{16,0},{20,4},{24,8},{28,12},{1,17},{... | collective-permute-start | bytes 319496 | tf_op jit(solution)/shard_map/cond/branch_1_fun/ppermute | solution.py:233
  50.2 5.8 %collective-permute-start.3 = (bf16[1,15,16,128]{3,2,1,0:T(8,128)(2,1)S(1)}, bf16[1,15,16,128]{3,2,1,0:T(8,128)(2,1)S(1)}, u32[]{:S(2)}, u32[]{:S(2)}) collective-permute-start(bf16[1,15,16,128]{3,2,1,0:T(8,128)(2,1)S(1)} %add_convert_fusion.12), channel_id=1, source_target_pairs={{0,2},{1,3},{2,0},{3,1},{4,6},{5,7},{6,4},{7,5},{8,10},{9,11},{10,... | collective-permute-start | bytes 184328 | tf_op jit(solution)/shard_map/cond/branch_1_fun/ppermute | solution.py:233
  52.2 5.4 %collective-permute-start.15 = (bf16[1,13,16,128]{3,2,1,0:T(8,128)(2,1)S(1)}, bf16[1,13,16,128]{3,2,1,0:T(8,128)(2,1)S(1)}, u32[]{:S(2)}, u32[]{:S(2)}) collective-permute-start(bf16[1,13,16,128]{3,2,1,0:T(8,128)(2,1)S(1)} %add_convert_fusion.14), channel_id=1, source_target_pairs={{0,2},{1,3},{2,0},{3,1},{4,6},{5,7},{6,4},{7,5},{8,10},{9,11},{10,... | collective-permute-start | bytes 159752 | tf_op jit(solution)/shard_map/cond/branch_1_fun/ppermute | solution.py:233
  56.0 4.3 %collective-permute-start.4 = (bf16[1,15,16,128]{3,2,1,0:T(8,128)(2,1)S(1)}, bf16[1,15,16,128]{3,2,1,0:T(8,128)(2,1)S(1)}, u32[]{:S(2)}, u32[]{:S(2)}) collective-permute-start(bf16[1,15,16,128]{3,2,1,0:T(8,128)(2,1)S(1)} %fusion.14), channel_id=1, source_target_pairs={{0,8},{4,12},{8,0},{12,4},{16,24},{20,28},{24,16},{28,20},{1,9},{5... | collective-permute-start | bytes 184328 | tf_op jit(solution)/shard_map/cond/branch_1_fun/ppermute | solution.py:233
  57.6 4.5 %collective-permute-start.16 = (bf16[1,13,16,128]{3,2,1,0:T(8,128)(2,1)S(1)}, bf16[1,13,16,128]{3,2,1,0:T(8,128)(2,1)S(1)}, u32[]{:S(2)}, u32[]{:S(2)}) collective-permute-start(bf16[1,13,16,128]{3,2,1,0:T(8,128)(2,1)S(1)} %fusion.15), channel_id=1, source_target_pairs={{0,8},{4,12},{8,0},{12,4},{16,24},{20,28},{24,16},{28,20},{1,9},{5... | collective-permute-start | bytes 159752 | tf_op jit(solution)/shard_map/cond/branch_1_fun/ppermute | solution.py:233
  61.0 24.6 %copy-start.4 = (bf16[1,15,16,128]{3,2,1,0:T(8,128)(2,1)}, bf16[1,15,16,128]{3,2,1,0:T(8,128)(2,1)S(1)}, u32[]{:S(2)}) copy-start(bf16[1,15,16,128]{3,2,1,0:T(8,128)(2,1)S(1)} %select_convert_fusion.2.refs_0_) | copy-start | bytes 184324 | tf_op jit(solution)/shard_map/cond
  61.0 5.2 %collective-permute-start.5 = (bf16[1,15,16,128]{3,2,1,0:T(8,128)(2,1)S(1)}, bf16[1,15,16,128]{3,2,1,0:T(8,128)(2,1)S(1)}, u32[]{:S(2)}, u32[]{:S(2)}) collective-permute-start(bf16[1,15,16,128]{3,2,1,0:T(8,128)(2,1)S(1)} %select_convert_fusion.2.refs_0_), channel_id=1, source_target_pairs={{0,2},{1,3},{2,0},{3,1},{4,6},{5,7},{6,4},{7,5},{8,10},{9,11},{10,... | collective-permute-start | bytes 184328 | tf_op jit(solution)/shard_map/cond/branch_1_fun/ppermute | solution.py:233
  62.8 9.4 %collective-permute-start.17 = (bf16[1,13,16,128]{3,2,1,0:T(8,128)(2,1)S(1)}, bf16[1,13,16,128]{3,2,1,0:T(8,128)(2,1)S(1)}, u32[]{:S(2)}, u32[]{:S(2)}) collective-permute-start(bf16[1,13,16,128]{3,2,1,0:T(8,128)(2,1)S(1)} %select_convert_fusion.3.refs_8_), channel_id=1, source_target_pairs={{0,2},{1,3},{2,0},{3,1},{4,6},{5,7},{6,4},{7,5},{8,10},{9,11},{10,... | collective-permute-start | bytes 159752 | tf_op jit(solution)/shard_map/cond/branch_1_fun/ppermute | solution.py:233
  66.2 7.5 %collective-permute-start.6 = (bf16[2,15,16,128]{3,2,1,0:T(8,128)(2,1)S(1)}, bf16[2,15,16,128]{3,2,1,0:T(8,128)(2,1)S(1)}, u32[]{:S(2)}, u32[]{:S(2)}) collective-permute-start(bf16[2,15,16,128]{3,2,1,0:T(8,128)(2,1)S(1)} %pad_maximum_fusion.8), channel_id=1, source_target_pairs={{0,1},{1,0},{2,3},{3,2},{4,5},{5,4},{6,7},{7,6},{8,9},{9,8},{10,11... | collective-permute-start | bytes 368648 | tf_op jit(solution)/shard_map/cond/branch_1_fun/ppermute | solution.py:233
  67.8 9.3 %collective-permute-start.24 = (bf16[32,32,128]{2,1,0:T(8,128)(2,1)S(1)}, bf16[32,32,128]{2,1,0:T(8,128)(2,1)S(1)}, u32[]{:S(2)}, u32[]{:S(2)}) collective-permute-start(bf16[32,32,128]{2,1,0:T(8,128)(2,1)S(1)} %get-tuple-element.141), channel_id=1, source_target_pairs={{1,2},{2,1},{5,6},{6,5},{9,10},{10,9},{13,14},{14,13},{17,18},{18,... | collective-permute-start | bytes 786440 | tf_op jit(solution)/shard_map/cond/branch_1_fun/ppermute | solution.py:276
  68.5 9.8 %collective-permute-start.25 = (bf16[32,32,128]{2,1,0:T(8,128)(2,1)S(1)}, bf16[32,32,128]{2,1,0:T(8,128)(2,1)S(1)}, u32[]{:S(2)}, u32[]{:S(2)}) collective-permute-start(bf16[32,32,128]{2,1,0:T(8,128)(2,1)S(1)} %get-tuple-element.142), channel_id=1, source_target_pairs={{0,1},{1,0},{2,3},{3,2},{4,5},{5,4},{6,7},{7,6},{8,9},{9,8},{10,11... | collective-permute-start | bytes 786440 | tf_op jit(solution)/shard_map/cond/branch_1_fun/ppermute | solution.py:233
  72.2 4.8 %collective-permute-start.18 = (bf16[2,13,16,128]{3,2,1,0:T(8,128)(2,1)S(1)}, bf16[2,13,16,128]{3,2,1,0:T(8,128)(2,1)S(1)}, u32[]{:S(2)}, u32[]{:S(2)}) collective-permute-start(bf16[2,13,16,128]{3,2,1,0:T(8,128)(2,1)S(1)} %pad_maximum_fusion.9), channel_id=1, source_target_pairs={{0,16},{4,20},{8,24},{12,28},{16,0},{20,4},{24,8},{28,12},{1,17},{... | collective-permute-start | bytes 319496 | tf_op jit(solution)/shard_map/cond/branch_1_fun/ppermute | solution.py:233
  73.8 9.1 %collective-permute-start.7 = (bf16[4,15,16,128]{3,2,1,0:T(8,128)(2,1)S(1)}, bf16[4,15,16,128]{3,2,1,0:T(8,128)(2,1)S(1)}, u32[]{:S(2)}, u32[]{:S(2)}) collective-permute-start(bf16[4,15,16,128]{3,2,1,0:T(8,128)(2,1)S(1)} %pad_maximum_fusion.6), channel_id=1, source_target_pairs={{0,16},{4,20},{8,24},{12,28},{16,0},{20,4},{24,8},{28,12},{1,17},{... | collective-permute-start | bytes 737288 | tf_op jit(solution)/shard_map/cond/branch_1_fun/ppermute | solution.py:233
  77.0 5.9 %collective-permute-start.19 = (bf16[4,13,16,128]{3,2,1,0:T(8,128)(2,1)S(1)}, bf16[4,13,16,128]{3,2,1,0:T(8,128)(2,1)S(1)}, u32[]{:S(2)}, u32[]{:S(2)}) collective-permute-start(bf16[4,13,16,128]{3,2,1,0:T(8,128)(2,1)S(1)} %pad_maximum_fusion.7), channel_id=1, source_target_pairs={{0,1},{1,0},{2,3},{3,2},{4,5},{5,4},{6,7},{7,6},{8,9},{9,8},{10,11... | collective-permute-start | bytes 638984 | tf_op jit(solution)/shard_map/cond/branch_1_fun/ppermute | solution.py:233
  77.1 6.5 %collective-permute-start.20 = (bf16[1,13,16,128]{3,2,1,0:T(8,128)(2,1)S(1)}, bf16[1,13,16,128]{3,2,1,0:T(8,128)(2,1)S(1)}, u32[]{:S(2)}, u32[]{:S(2)}) collective-permute-start(bf16[1,13,16,128]{3,2,1,0:T(8,128)(2,1)S(1)} %select_convert_fusion.3.refs_8_), channel_id=1, source_target_pairs={{0,4},{4,0},{8,12},{12,8},{16,20},{20,16},{24,28},{28,24},{1,5},{5... | collective-permute-start | bytes 159752 | tf_op jit(solution)/shard_map/cond/branch_1_fun/ppermute | solution.py:233
  77.1 6.6 %collective-permute-start.21 = (bf16[1,13,16,128]{3,2,1,0:T(8,128)(2,1)S(1)}, bf16[1,13,16,128]{3,2,1,0:T(8,128)(2,1)S(1)}, u32[]{:S(2)}, u32[]{:S(2)}) collective-permute-start(bf16[1,13,16,128]{3,2,1,0:T(8,128)(2,1)S(1)} %collective-permute-done.17.refs_9_), channel_id=1, source_target_pairs={{0,4},{4,0},{8,12},{12,8},{16,20},{20,16},{24,28},{28,24},{1,5},{5... | collective-permute-start | bytes 159752 | tf_op jit(solution)/shard_map/cond/branch_1_fun/ppermute | solution.py:233
  78.4 5.8 %collective-permute-start.8 = (bf16[1,15,16,128]{3,2,1,0:T(8,128)(2,1)S(1)}, bf16[1,15,16,128]{3,2,1,0:T(8,128)(2,1)S(1)}, u32[]{:S(2)}, u32[]{:S(2)}) collective-permute-start(bf16[1,15,16,128]{3,2,1,0:T(8,128)(2,1)S(1)} %select_convert_fusion.2.refs_0_), channel_id=1, source_target_pairs={{0,4},{4,0},{8,12},{12,8},{16,20},{20,16},{24,28},{28,24},{1,5},{5... | collective-permute-start | bytes 184328 | tf_op jit(solution)/shard_map/cond/branch_1_fun/ppermute | solution.py:233
  82.9 2.7 %collective-permute-start.23 = (bf16[4,13,16,128]{3,2,1,0:T(8,128)(2,1)S(1)}, bf16[4,13,16,128]{3,2,1,0:T(8,128)(2,1)S(1)}, u32[]{:S(2)}, u32[]{:S(2)}) collective-permute-start(bf16[4,13,16,128]{3,2,1,0:T(8,128)(2,1)S(1)} %collective-permute-done.19.refs_11_), channel_id=1, source_target_pairs={{0,4},{4,0},{8,12},{12,8},{16,20},{20,16},{24,28},{28,24},{1,5},{5... | collective-permute-start | bytes 638984 | tf_op jit(solution)/shard_map/cond/branch_1_fun/ppermute | solution.py:233
  82.9 2.6 %collective-permute-start.11 = (bf16[4,15,16,128]{3,2,1,0:T(8,128)(2,1)S(1)}, bf16[4,15,16,128]{3,2,1,0:T(8,128)(2,1)S(1)}, u32[]{:S(2)}, u32[]{:S(2)}) collective-permute-start(bf16[4,15,16,128]{3,2,1,0:T(8,128)(2,1)S(1)} %collective-permute-done.7.refs_3_), channel_id=1, source_target_pairs={{0,4},{4,0},{8,12},{12,8},{16,20},{20,16},{24,28},{28,24},{1,5},{5... | collective-permute-start | bytes 737288 | tf_op jit(solution)/shard_map/cond/branch_1_fun/ppermute | solution.py:233
  83.6 1.5 %collective-permute-start.22 = (bf16[2,13,16,128]{3,2,1,0:T(8,128)(2,1)S(1)}, bf16[2,13,16,128]{3,2,1,0:T(8,128)(2,1)S(1)}, u32[]{:S(2)}, u32[]{:S(2)}) collective-permute-start(bf16[2,13,16,128]{3,2,1,0:T(8,128)(2,1)S(1)} %collective-permute-done.18.refs_10_), channel_id=1, source_target_pairs={{0,4},{4,0},{8,12},{12,8},{16,20},{20,16},{24,28},{28,24},{1,5},{5... | collective-permute-start | bytes 319496 | tf_op jit(solution)/shard_map/cond/branch_1_fun/ppermute | solution.py:233
  83.8 1.3 %collective-permute-start.9 = (bf16[1,15,16,128]{3,2,1,0:T(8,128)(2,1)S(1)}, bf16[1,15,16,128]{3,2,1,0:T(8,128)(2,1)S(1)}, u32[]{:S(2)}, u32[]{:S(2)}) collective-permute-start(bf16[1,15,16,128]{3,2,1,0:T(8,128)(2,1)S(1)} %collective-permute-done.5.refs_1_), channel_id=1, source_target_pairs={{0,4},{4,0},{8,12},{12,8},{16,20},{20,16},{24,28},{28,24},{1,5},{5... | collective-permute-start | bytes 184328 | tf_op jit(solution)/shard_map/cond/branch_1_fun/ppermute | solution.py:233
  84.2 1.3 %collective-permute-start.10 = (bf16[2,15,16,128]{3,2,1,0:T(8,128)(2,1)S(1)}, bf16[2,15,16,128]{3,2,1,0:T(8,128)(2,1)S(1)}, u32[]{:S(2)}, u32[]{:S(2)}) collective-permute-start(bf16[2,15,16,128]{3,2,1,0:T(8,128)(2,1)S(1)} %collective-permute-done.6.refs_2_), channel_id=1, source_target_pairs={{0,4},{4,0},{8,12},{12,8},{16,20},{20,16},{24,28},{28,24},{1,5},{5... | collective-permute-start | bytes 368648 | tf_op jit(solution)/shard_map/cond/branch_1_fun/ppermute | solution.py:233
  (17 other events, 92.0 us)
